TPU v7x, 512 devices: a whole 4x8x8 slice. The times are simulated.
512 devices in a mesh: ctx: 64 (over x, y_lo, z), fsdp: 8 (over y_hi, core).
Axes of the slice: x: 4, y: 8 (y_hi: 4, y_lo: 2; y = y_hi * 2 + y_lo), z: 8, core: 2. Of those that a mesh axis runs over, the one named last changes fastest.
Arguments:
- queries: bfloat16 [2, 16384, 2048], P(None, 'ctx', 'fsdp'), may hold values from -5.5 to 5.5
- keys_values: bfloat16 [2, 2, 16384, 2048], P(None, None, 'ctx', 'fsdp'), may hold values from -5.5 to 5.5
- block_mask: int32 [256, 32], P('ctx'), may hold values 0 or 1
- out_weight: bfloat16 [2048, 4096], P('fsdp'), may hold values from -3 to 3
Outputs:
- mixed: bfloat16 [2, 16384, 4096], P(None, 'ctx', 'fsdp')
All inputs are finite; a program needn't handle non-finite values. No bound on the sum of `block_mask` on one device may be relied on, other than what follows from the above.
Results may differ from a plain program's by a relative error of at most 0.0058.
Values may be sent and summed in bfloat16 or wider, within the bound.
A program may use at most 64 MiB of HBM per device.

v0:
```python
import math
import jax
import jax.numpy as jnp
from jax import lax
from jax.sharding import PartitionSpec as P

HD = 128
BLK = 64
WINB = 32


def passed_along(array, axis, by):
    devices = lax.axis_size(axis)
    pairs = [(i, i + by) for i in range(devices) if 0 <= i + by < devices]
    return lax.ppermute(array, axis, pairs)


def block_rules(first_block, query_count, key_start, key_count, mask_rows):
    query_blocks = first_block + jnp.arange(query_count, dtype=jnp.int32)
    key_blocks = key_start + jnp.arange(key_count, dtype=jnp.int32)
    block_gap = query_blocks[:, None] - key_blocks[None, :]
    present = key_blocks[None, :] >= 0
    clean_ok = (block_gap >= 0) & (block_gap < WINB) & present
    offsets = jnp.arange(WINB, dtype=jnp.int32)
    picked = ((block_gap - 1)[:, :, None] == offsets[None, None, :]) & (mask_rows[:, None, :] == 1)
    noisy_ok = jnp.any(picked, axis=2) & present
    own_block = query_blocks[:, None] == query_blocks[None, :]

    def widen(table):
        return jnp.repeat(jnp.repeat(table, BLK, axis=0), BLK, axis=1)

    return (widen(clean_ok), widen(noisy_ok), widen(own_block))


def attend(query, keys, values, allowed):
    count, width = query.shape
    heads = width // HD
    query_three = query.reshape(count, heads, HD)
    key_three = keys.reshape(-1, heads, HD)
    value_three = values.reshape(-1, heads, HD)
    scores = jnp.einsum(
        "qhd,khd->hqk", query_three, key_three, preferred_element_type=jnp.float32
    ) * (1.0 / math.sqrt(HD))
    scores = jnp.where(allowed[None], scores, jnp.float32(-1e30))
    top = jnp.max(scores, axis=-1, keepdims=True)
    expo = jnp.exp(scores - top)
    weights = (expo / jnp.sum(expo, axis=-1, keepdims=True)).astype(jnp.bfloat16)
    result = jnp.einsum("hqk,khd->qhd", weights, value_three, preferred_element_type=jnp.float32)
    return result.reshape(count, width).astype(jnp.bfloat16)


def on_device(queries, keys_values, block_mask, out_weight):
    tokens = queries.shape[1]
    blocks_here = tokens // BLK
    reach = WINB * BLK // tokens
    own = keys_values[:, 0]
    pieces = []
    moving = own
    for step in range(reach):
        moving = passed_along(moving, "ctx", 1)
        pieces.insert(0, moving)
    window = jnp.concatenate(pieces + [own], axis=1)
    first_block = lax.axis_index("ctx") * blocks_here
    clean_ok, noisy_ok, own_ok = block_rules(
        first_block, blocks_here, first_block - WINB, blocks_here + WINB, block_mask
    )
    clean_out = attend(queries[0], window[0], window[1], clean_ok)
    noisy_keys = jnp.concatenate([window[0], keys_values[0, 1]], axis=0)
    noisy_values = jnp.concatenate([window[1], keys_values[1, 1]], axis=0)
    noisy_allowed = jnp.concatenate([noisy_ok, own_ok], axis=1)
    noisy_out = attend(queries[1], noisy_keys, noisy_values, noisy_allowed)
    attended = jnp.stack([clean_out, noisy_out])
    panel = lax.all_to_all(out_weight, "fsdp", split_axis=1, concat_axis=0, tiled=True)
    piece = lax.all_gather(attended, "fsdp", axis=2, tiled=True)
    columns = piece.shape[2]
    mixed = jnp.dot(piece.reshape(-1, columns), panel, preferred_element_type=jnp.float32)
    return mixed.astype(jnp.bfloat16).reshape(2, tokens, panel.shape[1])


def solution(mesh):
    in_specs = (
        P(None, "ctx", "fsdp"),
        P(None, None, "ctx", "fsdp"),
        P("ctx", None),
        P("fsdp", None),
    )
    out_specs = P(None, "ctx", "fsdp")
    return jax.shard_map(
        on_device, mesh=mesh, in_specs=in_specs, out_specs=out_specs, check_vma=False
    )
```

profile of v0, /device:TPU:1, one launch (start us, length us, event | category | flops | bytes accessed | tf_op | source)
XLA Modules:
  0.0 229.4 jit_solution(5361212706410624374)
XLA Ops:
  7.6 4.8 %collective-permute-start = (bf16[2,256,256]{1,2,0:T(8,128)(2,1)S(1)}, bf16[2,256,256]{1,2,0:T(8,128)(2,1)S(1)}, u32[]{:S(2)}, u32[]{:S(2)}) collective-permute-start(bf16[2,256,256]{1,2,0:T(8,128)(2,1)S(1)} %bitcast.72), channel_id=1, source_target_pairs={{0,8},{8,16},{16,24},{24,32},{32,40},{40,48},{48,56},{56,64},{64,7... | collective-permute-start | bytes 786440 | tf_op jit(solution)/shard_map/ppermute | solution.py:15
  12.5 3.3 %collective-permute-done = bf16[2,256,256]{1,2,0:T(8,128)(2,1)S(1)} collective-permute-done((bf16[2,256,256]{1,2,0:T(8,128)(2,1)S(1)}, bf16[2,256,256]{1,2,0:T(8,128)(2,1)S(1)}, u32[]{:S(2)}, u32[]{:S(2)}) %collective-permute-start) | collective-permute-done | bytes 262176 | tf_op jit(solution)/shard_map/ppermute | solution.py:15
  15.8 5.7 %collective-permute-start.1 = (bf16[2,256,256]{1,2,0:T(8,128)(2,1)S(1)}, bf16[2,256,256]{1,2,0:T(8,128)(2,1)S(1)}, u32[]{:S(2)}, u32[]{:S(2)}) collective-permute-start(bf16[2,256,256]{1,2,0:T(8,128)(2,1)S(1)} %collective-permute-done), channel_id=1, source_target_pairs={{0,8},{8,16},{16,24},{24,32},{32,40},{40,48},{48,56},{56,64},{64,7... | collective-permute-start | bytes 786440 | tf_op jit(solution)/shard_map/ppermute | solution.py:15
  21.4 3.3 %collective-permute-done.1 = bf16[2,256,256]{1,2,0:T(8,128)(2,1)S(1)} collective-permute-done((bf16[2,256,256]{1,2,0:T(8,128)(2,1)S(1)}, bf16[2,256,256]{1,2,0:T(8,128)(2,1)S(1)}, u32[]{:S(2)}, u32[]{:S(2)}) %collective-permute-start.1) | collective-permute-done | bytes 262176 | tf_op jit(solution)/shard_map/ppermute | solution.py:15
  24.7 5.5 %collective-permute-start.2 = (bf16[2,256,256]{1,2,0:T(8,128)(2,1)S(1)}, bf16[2,256,256]{1,2,0:T(8,128)(2,1)}, u32[]{:S(2)}, u32[]{:S(2)}) collective-permute-start(bf16[2,256,256]{1,2,0:T(8,128)(2,1)S(1)} %collective-permute-done.1), channel_id=1, source_target_pairs={{0,8},{8,16},{16,24},{24,32},{32,40},{40,48},{48,56},{56,64},{64,7... | collective-permute-start | bytes 786440 | tf_op jit(solution)/shard_map/ppermute | solution.py:15
  30.3 4.1 %copy.58 = bf16[256,4096]{0,1:T(8,128)(2,1)} copy(bf16[256,4096]{1,0:T(8,128)(2,1)} %param.7) | data formatting | bytes 4194304 | tf_op args[3]
  34.4 10.1 %all-to-all-start = ((bf16[256,8,512]{0,2,1:T(8,128)(2,1)}), bf16[256,8,512]{0,2,1:T(8,128)(2,1)S(1)}, u32[]{:S(2)}, u32[]{:S(2)}) async-start(bf16[256,8,512]{0,2,1:T(8,128)(2,1)} %bitcast.64), calls=%async_computation | async-start | bytes 4194304 | tf_op jit(solution)/shard_map/all_to_all | solution.py:73
  44.5 4.3 %collective-permute-start.3 = (bf16[2,256,256]{1,2,0:T(8,128)(2,1)}, bf16[2,256,256]{1,2,0:T(8,128)(2,1)S(1)}, u32[]{:S(2)}, u32[]{:S(2)}) collective-permute-start(bf16[2,256,256]{1,2,0:T(8,128)(2,1)} %collective-permute-done.2), channel_id=1, source_target_pairs={{0,8},{8,16},{16,24},{24,32},{32,40},{40,48},{48,56},{56,64},{64,7... | collective-permute-start | bytes 786440 | tf_op jit(solution)/shard_map/ppermute | solution.py:15
  48.9 5.9 %collective-permute-done.3 = bf16[2,256,256]{1,2,0:T(8,128)(2,1)S(1)} collective-permute-done((bf16[2,256,256]{1,2,0:T(8,128)(2,1)}, bf16[2,256,256]{1,2,0:T(8,128)(2,1)S(1)}, u32[]{:S(2)}, u32[]{:S(2)}) %collective-permute-start.3) | collective-permute-done | bytes 262176 | tf_op jit(solution)/shard_map/ppermute | solution.py:15
  54.8 5.3 %collective-permute-start.4 = (bf16[2,256,256]{1,2,0:T(8,128)(2,1)S(1)}, bf16[2,256,256]{1,2,0:T(8,128)(2,1)S(1)}, u32[]{:S(2)}, u32[]{:S(2)}) collective-permute-start(bf16[2,256,256]{1,2,0:T(8,128)(2,1)S(1)} %collective-permute-done.3), channel_id=1, source_target_pairs={{0,8},{8,16},{16,24},{24,32},{32,40},{40,48},{48,56},{56,64},{64,7... | collective-permute-start | bytes 786440 | tf_op jit(solution)/shard_map/ppermute | solution.py:15
  60.2 4.6 %collective-permute-done.4 = bf16[2,256,256]{1,2,0:T(8,128)(2,1)S(1)} collective-permute-done((bf16[2,256,256]{1,2,0:T(8,128)(2,1)S(1)}, bf16[2,256,256]{1,2,0:T(8,128)(2,1)S(1)}, u32[]{:S(2)}, u32[]{:S(2)}) %collective-permute-start.4) | collective-permute-done | bytes 262176 | tf_op jit(solution)/shard_map/ppermute | solution.py:15
  64.8 6.0 %collective-permute-start.5 = (bf16[2,256,256]{1,2,0:T(8,128)(2,1)S(1)}, bf16[2,256,256]{1,2,0:T(8,128)(2,1)}, u32[]{:S(2)}, u32[]{:S(2)}) collective-permute-start(bf16[2,256,256]{1,2,0:T(8,128)(2,1)S(1)} %collective-permute-done.4), channel_id=1, source_target_pairs={{0,8},{8,16},{16,24},{24,32},{32,40},{40,48},{48,56},{56,64},{64,7... | collective-permute-start | bytes 786440 | tf_op jit(solution)/shard_map/ppermute | solution.py:15
  71.0 3.0 %collective-permute-done.5 = bf16[2,256,256]{1,2,0:T(8,128)(2,1)} collective-permute-done((bf16[2,256,256]{1,2,0:T(8,128)(2,1)S(1)}, bf16[2,256,256]{1,2,0:T(8,128)(2,1)}, u32[]{:S(2)}, u32[]{:S(2)}) %collective-permute-start.5) | collective-permute-done | bytes 262176 | tf_op jit(solution)/shard_map/ppermute | solution.py:15
  74.0 4.2 %collective-permute-start.6 = (bf16[2,256,256]{1,2,0:T(8,128)(2,1)}, bf16[2,256,256]{1,2,0:T(8,128)(2,1)S(1)}, u32[]{:S(2)}, u32[]{:S(2)}) collective-permute-start(bf16[2,256,256]{1,2,0:T(8,128)(2,1)} %collective-permute-done.5), channel_id=1, source_target_pairs={{0,8},{8,16},{16,24},{24,32},{32,40},{40,48},{48,56},{56,64},{64,7... | collective-permute-start | bytes 786440 | tf_op jit(solution)/shard_map/ppermute | solution.py:15
  82.9 4.1 %collective-permute-start.7 = (bf16[2,256,256]{1,2,0:T(8,128)(2,1)S(1)}, bf16[2,256,256]{1,2,0:T(8,128)(2,1)S(1)}, u32[]{:S(2)}, u32[]{:S(2)}) collective-permute-start(bf16[2,256,256]{1,2,0:T(8,128)(2,1)S(1)} %collective-permute-done.6), channel_id=1, source_target_pairs={{0,8},{8,16},{16,24},{24,32},{32,40},{40,48},{48,56},{56,64},{64,7... | collective-permute-start | bytes 786440 | tf_op jit(solution)/shard_map/ppermute | solution.py:15
  89.0 1.3 collective-permute-done.7
  93.6 1.4 copy.51
  96.0 2.9 %fusion.58 = f32[2,256]{1,0:T(2,128)S(1)} fusion(bf16[2304,2,128]{0,2,1:T(8,128)(2,1)S(1)} %bitcast.66, bf16[256,2,128]{0,2,1:T(8,128)(2,1)S(1)} %bitcast.77, pred[256,2304]{0,1:T(8,128)(4,1)} %bitcast.73), kind=kOutput, calls=%fused_computation.66 | convolution fusion | flops 306710784 | bytes 1902592 | tf_op jit(solution)/shard_map/sub | solution.py:46
  98.9 4.4 %fusion.15 = bf16[2,128,256]{2,1,0:T(8,128)(2,1)} fusion(bf16[2304,2,128]{0,2,1:T(8,128)(2,1)} %bitcast.70, f32[2,256]{1,0:T(2,128)S(1)} %fusion.58, bf16[2304,2,128]{0,2,1:T(8,128)(2,1)S(1)} %bitcast.67, bf16[256,2,128]{0,2,1:T(8,128)(2,1)S(1)} %bitcast.78, pred[256,2304]{0,1:T(8,128)(4,1)} %bitcast.74), kind=kOutput, calls=%fused_computation.22 | convolution fusion | flops 609946368 | bytes 3213312 | tf_op jit(solution)/shard_map/hqk,khd->qhd/dot_general | solution.py:48
  104.4 3.4 %exponential_reduce_fusion = f32[2,256]{1,0:T(2,128)S(1)} fusion(bf16[256,2,128]{0,2,1:T(8,128)(2,1)} %bitcast.79, pred[256,2560]{0,1:T(8,128)(4,1)} %pad_add_fusion, bf16[256,2,128]{2,0,1:T(8,128)(2,1)S(1)} %copy-done.12, bf16[2304,2,128]{2,0,1:T(8,128)(2,1)} %copy.51), kind=kOutput, calls=%fused_computation.7 | convolution fusion | flops 343411200 | bytes 2099200 | tf_op jit(solution)/shard_map/sub | solution.py:46
  107.8 4.5 %fusion.16 = bf16[2,128,256]{2,1,0:T(8,128)(2,1)} fusion(f32[2,256]{1,0:T(2,128)S(1)} %exponential_reduce_fusion, bf16[256,2,128]{0,2,1:T(8,128)(2,1)} %bitcast.81, bf16[2304,2,128]{0,2,1:T(8,128)(2,1)} %bitcast.71, bf16[256,2,128]{0,2,1:T(8,128)(2,1)} %bitcast.80, pred[256,2560]{0,1:T(8,128)(4,1)} %pad_add_fusion, bf16[256,2,128]{2,0,1:T(8,128)(2,1)S(1)} %copy-done.12, ...), kind=kOutput, calls=%fused_computation.23 | convolution fusion | flops 682953728 | bytes 3540992 | tf_op jit(solution)/shard_map/hqk,khd->qhd/dot_general | solution.py:48
  114.1 2.4 %copy.59 = bf16[8,256,512]{2,1,0:T(8,128)(2,1)} copy(bf16[8,256,512]{1,2,0:T(8,128)(2,1)S(1)} %bitcast.63) | data formatting | bytes 4194304 | tf_op jit(solution)/shard_map/all_to_all | solution.py:73
  116.5 101.8 %all-gather.2.cloned.1.call-done = bf16[2,256,2048]{2,1,0:T(8,128)(2,1)} async-done(((bf16[2,256,256]{2,1,0:T(8,128)(2,1)}), bf16[2,256,2048]{2,1,0:T(8,128)(2,1)}) %all-gather.2.cloned.1.call-update) | async-done | bytes 2097168 | tf_op jit(solution)/shard_map/all_gather | solution.py:74
  218.3 4.3 %convolution_convert_fusion = bf16[512,512]{1,0:T(8,128)(2,1)} fusion(bf16[512,2048]{1,0:T(8,128)(2,1)} %bitcast.84, bf16[2048,512]{1,0:T(8,128)(2,1)} %bitcast.69), kind=kOutput, calls=%fused_computation.21 | convolution fusion | flops 1074003968 | bytes 4718592 | tf_op jit(solution)/shard_map/dot_general | solution.py:76
  (75 shorter events, 15.0 us)
Async XLA Ops:
  7.6 8.1 %collective-permute-start = (bf16[2,256,256]{1,2,0:T(8,128)(2,1)S(1)}, bf16[2,256,256]{1,2,0:T(8,128)(2,1)S(1)}, u32[]{:S(2)}, u32[]{:S(2)}) collective-permute-start(bf16[2,256,256]{1,2,0:T(8,128)(2,1)S(1)} %bitcast.72), channel_id=1, source_target_pairs={{0,8},{8,16},{16,24},{24,32},{32,40},{40,48},{48,56},{56,64},{64,7... | collective-permute-start | bytes 786440 | tf_op jit(solution)/shard_map/ppermute | solution.py:15
  15.8 18.6 %copy-start.3 = (bf16[2,256,256]{1,2,0:T(8,128)(2,1)}, bf16[2,256,256]{1,2,0:T(8,128)(2,1)S(1)}, u32[]{:S(2)}) copy-start(bf16[2,256,256]{1,2,0:T(8,128)(2,1)S(1)} %collective-permute-done) | copy-start | bytes 786436
  15.8 8.9 %collective-permute-start.1 = (bf16[2,256,256]{1,2,0:T(8,128)(2,1)S(1)}, bf16[2,256,256]{1,2,0:T(8,128)(2,1)S(1)}, u32[]{:S(2)}, u32[]{:S(2)}) collective-permute-start(bf16[2,256,256]{1,2,0:T(8,128)(2,1)S(1)} %collective-permute-done), channel_id=1, source_target_pairs={{0,8},{8,16},{16,24},{24,32},{32,40},{40,48},{48,56},{56,64},{64,7... | collective-permute-start | bytes 786440 | tf_op jit(solution)/shard_map/ppermute | solution.py:15
  24.7 9.6 %copy-start.5 = (bf16[2,256,256]{1,2,0:T(8,128)(2,1)}, bf16[2,256,256]{1,2,0:T(8,128)(2,1)S(1)}, u32[]{:S(2)}) copy-start(bf16[2,256,256]{1,2,0:T(8,128)(2,1)S(1)} %collective-permute-done.1) | copy-start | bytes 786436
  24.7 19.7 %collective-permute-start.2 = (bf16[2,256,256]{1,2,0:T(8,128)(2,1)S(1)}, bf16[2,256,256]{1,2,0:T(8,128)(2,1)}, u32[]{:S(2)}, u32[]{:S(2)}) collective-permute-start(bf16[2,256,256]{1,2,0:T(8,128)(2,1)S(1)} %collective-permute-done.1), channel_id=1, source_target_pairs={{0,8},{8,16},{16,24},{24,32},{32,40},{40,48},{48,56},{56,64},{64,7... | collective-permute-start | bytes 786440 | tf_op jit(solution)/shard_map/ppermute | solution.py:15
  34.3 25.8 %copy-start.13 = (s32[4,32]{1,0:T(4,128)S(1)}, s32[4,32]{1,0:T(4,128)}, u32[]{:S(2)}) copy-start(s32[4,32]{1,0:T(4,128)} %param.6) | copy-start | bytes 1540
  34.3 36.6 %copy-start.2 = (bf16[2,256,256]{2,1,0:T(8,128)(2,1)S(1)}, bf16[2,256,256]{2,1,0:T(8,128)(2,1)}, u32[]{:S(2)}) copy-start(bf16[2,256,256]{2,1,0:T(8,128)(2,1)} %param.4) | copy-start | bytes 786436
  34.3 46.1 %copy-start.1 = (bf16[2,2,256,256]{3,2,1,0:T(8,128)(2,1)S(1)}, bf16[2,2,256,256]{3,2,1,0:T(8,128)(2,1)}, u32[]{:S(2)}) copy-start(bf16[2,2,256,256]{3,2,1,0:T(8,128)(2,1)} %param.5) | copy-start | bytes 1572868
  34.4 79.7 %all-to-all-start = ((bf16[256,8,512]{0,2,1:T(8,128)(2,1)}), bf16[256,8,512]{0,2,1:T(8,128)(2,1)S(1)}, u32[]{:S(2)}, u32[]{:S(2)}) async-start(bf16[256,8,512]{0,2,1:T(8,128)(2,1)} %bitcast.64), calls=%async_computation | async-start | bytes 4194304 | tf_op jit(solution)/shard_map/all_to_all | solution.py:73
  44.5 173.8 %all-gather.2.cloned.1.call-start = ((), (), s32[]{:S(2)}) async-start(), calls=%async_computation.1 | async-start | bytes 2359296 | tf_op jit(solution)/shard_map/all_gather | solution.py:74
  44.5 10.3 %collective-permute-start.3 = (bf16[2,256,256]{1,2,0:T(8,128)(2,1)}, bf16[2,256,256]{1,2,0:T(8,128)(2,1)S(1)}, u32[]{:S(2)}, u32[]{:S(2)}) collective-permute-start(bf16[2,256,256]{1,2,0:T(8,128)(2,1)} %collective-permute-done.2), channel_id=1, source_target_pairs={{0,8},{8,16},{16,24},{24,32},{32,40},{40,48},{48,56},{56,64},{64,7... | collective-permute-start | bytes 786440 | tf_op jit(solution)/shard_map/ppermute | solution.py:15
  54.8 16.1 %copy-start.7 = (bf16[2,256,256]{1,2,0:T(8,128)(2,1)}, bf16[2,256,256]{1,2,0:T(8,128)(2,1)S(1)}, u32[]{:S(2)}) copy-start(bf16[2,256,256]{1,2,0:T(8,128)(2,1)S(1)} %collective-permute-done.3) | copy-start | bytes 786436
  54.8 10.1 %collective-permute-start.4 = (bf16[2,256,256]{1,2,0:T(8,128)(2,1)S(1)}, bf16[2,256,256]{1,2,0:T(8,128)(2,1)S(1)}, u32[]{:S(2)}, u32[]{:S(2)}) collective-permute-start(bf16[2,256,256]{1,2,0:T(8,128)(2,1)S(1)} %collective-permute-done.3), channel_id=1, source_target_pairs={{0,8},{8,16},{16,24},{24,32},{32,40},{40,48},{48,56},{56,64},{64,7... | collective-permute-start | bytes 786440 | tf_op jit(solution)/shard_map/ppermute | solution.py:15
  64.8 6.1 %copy-start.9 = (bf16[2,256,256]{1,2,0:T(8,128)(2,1)}, bf16[2,256,256]{1,2,0:T(8,128)(2,1)S(1)}, u32[]{:S(2)}) copy-start(bf16[2,256,256]{1,2,0:T(8,128)(2,1)S(1)} %collective-permute-done.4) | copy-start | bytes 786436
  64.8 9.2 %collective-permute-start.5 = (bf16[2,256,256]{1,2,0:T(8,128)(2,1)S(1)}, bf16[2,256,256]{1,2,0:T(8,128)(2,1)}, u32[]{:S(2)}, u32[]{:S(2)}) collective-permute-start(bf16[2,256,256]{1,2,0:T(8,128)(2,1)S(1)} %collective-permute-done.4), channel_id=1, source_target_pairs={{0,8},{8,16},{16,24},{24,32},{32,40},{40,48},{48,56},{56,64},{64,7... | collective-permute-start | bytes 786440 | tf_op jit(solution)/shard_map/ppermute | solution.py:15
  74.0 8.9 %collective-permute-start.6 = (bf16[2,256,256]{1,2,0:T(8,128)(2,1)}, bf16[2,256,256]{1,2,0:T(8,128)(2,1)S(1)}, u32[]{:S(2)}, u32[]{:S(2)}) collective-permute-start(bf16[2,256,256]{1,2,0:T(8,128)(2,1)} %collective-permute-done.5), channel_id=1, source_target_pairs={{0,8},{8,16},{16,24},{24,32},{32,40},{40,48},{48,56},{56,64},{64,7... | collective-permute-start | bytes 786440 | tf_op jit(solution)/shard_map/ppermute | solution.py:15
  80.5 10.8 %copy-start.10 = (bf16[2,256,256]{1,2,0:T(8,128)(2,1)S(1)}, bf16[2,256,256]{1,2,0:T(8,128)(2,1)}, u32[]{:S(2)}) copy-start(bf16[2,256,256]{1,2,0:T(8,128)(2,1)} %copy-done.9) | copy-start | bytes 786436
  81.4 10.0 %copy-start.8 = (bf16[2,256,256]{1,2,0:T(8,128)(2,1)S(1)}, bf16[2,256,256]{1,2,0:T(8,128)(2,1)}, u32[]{:S(2)}) copy-start(bf16[2,256,256]{1,2,0:T(8,128)(2,1)} %copy-done.7) | copy-start | bytes 786436
  82.9 7.4 %collective-permute-start.7 = (bf16[2,256,256]{1,2,0:T(8,128)(2,1)S(1)}, bf16[2,256,256]{1,2,0:T(8,128)(2,1)S(1)}, u32[]{:S(2)}, u32[]{:S(2)}) collective-permute-start(bf16[2,256,256]{1,2,0:T(8,128)(2,1)S(1)} %collective-permute-done.6), channel_id=1, source_target_pairs={{0,8},{8,16},{16,24},{24,32},{32,40},{40,48},{48,56},{56,64},{64,7... | collective-permute-start | bytes 786440 | tf_op jit(solution)/shard_map/ppermute | solution.py:15
  87.9 4.5 %copy-start.6 = (bf16[2,256,256]{1,2,0:T(8,128)(2,1)S(1)}, bf16[2,256,256]{1,2,0:T(8,128)(2,1)}, u32[]{:S(2)}) copy-start(bf16[2,256,256]{1,2,0:T(8,128)(2,1)} %copy-done.5) | copy-start | bytes 786436
  87.9 4.5 %copy-start.4 = (bf16[2,256,256]{1,2,0:T(8,128)(2,1)S(1)}, bf16[2,256,256]{1,2,0:T(8,128)(2,1)}, u32[]{:S(2)}) copy-start(bf16[2,256,256]{1,2,0:T(8,128)(2,1)} %copy-done.3) | copy-start | bytes 786436
  93.6 2.4 %copy-start.11 = (bf16[1,256,256]{1,2,0:T(8,128)(2,1)S(1)}, bf16[1,256,256]{1,2,0:T(8,128)(2,1)}, u32[]{:S(2)}) copy-start(bf16[1,256,256]{1,2,0:T(8,128)(2,1)} %copy.66) | copy-start | bytes 393220
  98.9 5.4 %copy-start.12 = (bf16[256,2,128]{2,0,1:T(8,128)(2,1)S(1)}, bf16[256,2,128]{2,0,1:T(8,128)(2,1)}, u32[]{:S(2)}) copy-start(bf16[256,2,128]{2,0,1:T(8,128)(2,1)} %copy.52) | copy-start | bytes 393220
  104.4 3.4 %copy-start = (bf16[2304,2,128]{2,0,1:T(8,128)(2,1)S(1)}, bf16[2304,2,128]{2,0,1:T(8,128)(2,1)}, u32[]{:S(2)}) copy-start(bf16[2304,2,128]{2,0,1:T(8,128)(2,1)} %copy.51) | copy-start | bytes 3538948
Sparse Core Ops, SparseCore 0:
  114.2 104.0 all-gather.1
where the time goes:
time: 230 us; the launch traced here: 229 us
  waiting for transfers between devices  123 us (53%)
  starting transfers between devices  50.1 us (22%)
  local copies, waits for them, and re-layouts  20.7 us (9%)
  matrix products  19.5 us (8%)
  between operations  13.7 us (6%)
    all_gather x1, waiting for transfers between devices, on_device(): piece = lax.all_gather(attended, 'fsdp', axis=2, tiled=True)  102 us
    ppermute x8, starting transfers between devices, passed_along(): return lax.ppermute(array, axis, pairs)  40 us
    ppermute x8, waiting for transfers between devices, passed_along(): return lax.ppermute(array, axis, pairs)  21.4 us
    all_to_all x1, starting transfers between devices, on_device(): lax.all_to_all(out_weight, 'fsdp', split_axis=1, concat_axis=0, tiled=True)  10.1 us
    dot_general x2, matrix products, attend(): jnp.einsum('hqk,khd->qhd', weights, value_three, preferred_element_type=j...  8.93 us
    unnamed x41, local copies, waits for them, and re-layouts  7.94 us
    sub x2, matrix products, attend(): expo = jnp.exp(scores - top)  6.32 us
  transfers between devices with their start and end apart: 10, of which 7 were waited for; matrix products, arithmetic and copies ran while one was open for 16% of the time, Pallas kernels for 0%

commit v1 on v0

--- a/solution.py
+++ b/solution.py
@@ -71,7 +71,10 @@
     noisy_out = attend(queries[1], noisy_keys, noisy_values, noisy_allowed)
     attended = jnp.stack([clean_out, noisy_out])
     panel = lax.all_to_all(out_weight, "fsdp", split_axis=1, concat_axis=0, tiled=True)
-    piece = lax.all_gather(attended, "fsdp", axis=2, tiled=True)
+    size = lax.axis_size("fsdp")
+    blocks = jnp.stack([attended for _ in range(size)])
+    blocks = lax.all_to_all(blocks, "fsdp", split_axis=0, concat_axis=0)
+    piece = jnp.concatenate(blocks, axis=2)
     columns = piece.shape[2]
     mixed = jnp.dot(piece.reshape(-1, columns), panel, preferred_element_type=jnp.float32)
     return mixed.astype(jnp.bfloat16).reshape(2, tokens, panel.shape[1])

time: 230 us -> 238 us (1.035)
  the two profiles are of different devices: /device:TPU:1 before, /device:TPU:6 now
where the time goes in v1:
time: 238 us; the launch traced here: 237 us
  waiting for transfers between devices  163 us (68%)
  starting transfers between devices  29.2 us (12%)
  local copies, waits for them, and re-layouts  24.6 us (10%)
  matrix products  17.6 us (7%)
    ppermute x8, waiting for transfers between devices, passed_along(): return lax.ppermute(array, axis, pairs)  113 us
    all_to_all x1, waiting for transfers between devices, on_device(): blocks = lax.all_to_all(blocks, 'fsdp', split_axis=0, concat_axis=0)  49.8 us
    ppermute x8, starting transfers between devices, passed_along(): return lax.ppermute(array, axis, pairs)  17.7 us
    unnamed x46, local copies, waits for them, and re-layouts  9.5 us
    dot_general x2, matrix products, attend(): jnp.einsum('hqk,khd->qhd', weights, value_three, preferred_element_type=j...  9.34 us
    all_to_all x1, starting transfers between devices, on_device(): lax.all_to_all(out_weight, 'fsdp', split_axis=1, concat_axis=0, tiled=True)  6.35 us
    sub x2, matrix products, attend(): expo = jnp.exp(scores - top)  6.18 us
    all_to_all x1, starting transfers between devices, on_device(): blocks = lax.all_to_all(blocks, 'fsdp', split_axis=0, concat_axis=0)  5.21 us
  transfers between devices with their start and end apart: 10, of which 8 were waited for; matrix products, arithmetic and copies ran while one was open for 15% of the time, Pallas kernels for 0%

profile of v1, /device:TPU:6, one launch (start us, length us, event | category | flops | bytes accessed | tf_op | source)
XLA Modules:
  0.0 237.3 jit_solution(4489093504674853448)
XLA Ops:
  1.1 4.3 %collective-permute-start = (bf16[2,256,256]{1,2,0:T(8,128)(2,1)S(1)}, bf16[2,256,256]{1,2,0:T(8,128)(2,1)S(1)}, u32[]{:S(2)}, u32[]{:S(2)}) collective-permute-start(bf16[2,256,256]{1,2,0:T(8,128)(2,1)S(1)} %bitcast.77), channel_id=1, source_target_pairs={{0,8},{8,16},{16,24},{24,32},{32,40},{40,48},{48,56},{56,64},{64,7... | collective-permute-start | bytes 786440 | tf_op jit(solution)/shard_map/ppermute | solution.py:15
  5.4 14.2 %collective-permute-done = bf16[2,256,256]{1,2,0:T(8,128)(2,1)S(1)} collective-permute-done((bf16[2,256,256]{1,2,0:T(8,128)(2,1)S(1)}, bf16[2,256,256]{1,2,0:T(8,128)(2,1)S(1)}, u32[]{:S(2)}, u32[]{:S(2)}) %collective-permute-start) | collective-permute-done | bytes 262176 | tf_op jit(solution)/shard_map/ppermute | solution.py:15
  19.6 1.9 collective-permute-start.1
  21.6 10.5 %collective-permute-done.1 = bf16[2,256,256]{1,2,0:T(8,128)(2,1)S(1)} collective-permute-done((bf16[2,256,256]{1,2,0:T(8,128)(2,1)S(1)}, bf16[2,256,256]{1,2,0:T(8,128)(2,1)S(1)}, u32[]{:S(2)}, u32[]{:S(2)}) %collective-permute-start.1) | collective-permute-done | bytes 262176 | tf_op jit(solution)/shard_map/ppermute | solution.py:15
  32.0 1.9 collective-permute-start.2
  33.9 4.1 %copy.74 = bf16[256,4096]{0,1:T(8,128)(2,1)} copy(bf16[256,4096]{1,0:T(8,128)(2,1)} %param.7) | data formatting | bytes 4194304 | tf_op args[3]
  38.0 6.3 %all-to-all-start.1 = ((bf16[256,8,512]{0,2,1:T(8,128)(2,1)}), bf16[256,8,512]{0,2,1:T(8,128)(2,1)S(1)}, u32[]{:S(2)}, u32[]{:S(2)}) async-start(bf16[256,8,512]{0,2,1:T(8,128)(2,1)} %bitcast.67), calls=%async_computation.1 | async-start | bytes 4194304 | tf_op jit(solution)/shard_map/all_to_all | solution.py:73
  44.4 1.9 collective-permute-start.3
  46.4 55.1 %collective-permute-done.3 = bf16[2,256,256]{1,2,0:T(8,128)(2,1)S(1)} collective-permute-done((bf16[2,256,256]{1,2,0:T(8,128)(2,1)}, bf16[2,256,256]{1,2,0:T(8,128)(2,1)S(1)}, u32[]{:S(2)}, u32[]{:S(2)}) %collective-permute-start.3) | collective-permute-done | bytes 262176 | tf_op jit(solution)/shard_map/ppermute | solution.py:15
  103.6 11.0 %collective-permute-done.4 = bf16[2,256,256]{1,2,0:T(8,128)(2,1)S(1)} collective-permute-done((bf16[2,256,256]{1,2,0:T(8,128)(2,1)S(1)}, bf16[2,256,256]{1,2,0:T(8,128)(2,1)S(1)}, u32[]{:S(2)}, u32[]{:S(2)}) %collective-permute-start.4) | collective-permute-done | bytes 262176 | tf_op jit(solution)/shard_map/ppermute | solution.py:15
  114.6 1.9 collective-permute-start.5
  116.6 10.3 %collective-permute-done.5 = bf16[2,256,256]{1,2,0:T(8,128)(2,1)} collective-permute-done((bf16[2,256,256]{1,2,0:T(8,128)(2,1)S(1)}, bf16[2,256,256]{1,2,0:T(8,128)(2,1)}, u32[]{:S(2)}, u32[]{:S(2)}) %collective-permute-start.5) | collective-permute-done | bytes 262176 | tf_op jit(solution)/shard_map/ppermute | solution.py:15
  133.4 4.9 %collective-permute-done.6 = bf16[2,256,256]{1,2,0:T(8,128)(2,1)S(1)} collective-permute-done((bf16[2,256,256]{1,2,0:T(8,128)(2,1)}, bf16[2,256,256]{1,2,0:T(8,128)(2,1)S(1)}, u32[]{:S(2)}, u32[]{:S(2)}) %collective-permute-start.6) | collective-permute-done | bytes 262176 | tf_op jit(solution)/shard_map/ppermute | solution.py:15
  138.3 1.9 collective-permute-start.7
  142.3 7.4 %collective-permute-done.7 = bf16[2,256,256]{1,2,0:T(8,128)(2,1)S(1)} collective-permute-done((bf16[2,256,256]{1,2,0:T(8,128)(2,1)S(1)}, bf16[2,256,256]{1,2,0:T(8,128)(2,1)S(1)}, u32[]{:S(2)}, u32[]{:S(2)}) %collective-permute-start.7) | collective-permute-done | bytes 262176 | tf_op jit(solution)/shard_map/ppermute | solution.py:15
  154.3 3.3 %exponential_reduce_fusion = f32[2,256]{1,0:T(2,128)S(1)} fusion(bf16[256,2,128]{0,2,1:T(8,128)(2,1)S(1)} %bitcast.85, pred[256,2560]{0,1:T(8,128)(4,1)} %pad_add_fusion, bf16[256,2,128]{2,0,1:T(8,128)(2,1)S(1)} %copy-done.12, bf16[2304,2,128]{2,0,1:T(8,128)(2,1)} %copy.67), kind=kOutput, calls=%fused_computation.7 | convolution fusion | flops 343411200 | bytes 2099200 | tf_op jit(solution)/shard_map/sub | solution.py:46
  157.6 4.9 %fusion.16 = bf16[2,128,256]{2,1,0:T(8,128)(2,1)} fusion(f32[2,256]{1,0:T(2,128)S(1)} %exponential_reduce_fusion, bf16[256,2,128]{0,2,1:T(8,128)(2,1)} %bitcast.86, bf16[2304,2,128]{0,2,1:T(8,128)(2,1)} %bitcast.75, bf16[256,2,128]{0,2,1:T(8,128)(2,1)} %bitcast.84, pred[256,2560]{0,1:T(8,128)(4,1)} %pad_add_fusion, bf16[256,2,128]{2,0,1:T(8,128)(2,1)S(1)} %copy-done.12, ...), kind=kOutput, calls=%fused_computation.23 | convolution fusion | flops 682953728 | bytes 3540992 | tf_op jit(solution)/shard_map/hqk,khd->qhd/dot_general | solution.py:48
  163.5 2.9 %fusion.58 = f32[2,256]{1,0:T(2,128)S(1)} fusion(bf16[2304,2,128]{0,2,1:T(8,128)(2,1)S(1)} %bitcast.70, bf16[256,2,128]{0,2,1:T(8,128)(2,1)S(1)} %bitcast.82, pred[256,2304]{0,1:T(8,128)(4,1)} %bitcast.78), kind=kOutput, calls=%fused_computation.66 | convolution fusion | flops 306710784 | bytes 1902592 | tf_op jit(solution)/shard_map/sub | solution.py:46
  166.4 4.4 %fusion.15 = bf16[2,128,256]{2,1,0:T(8,128)(2,1)} fusion(bf16[2304,2,128]{0,2,1:T(8,128)(2,1)} %bitcast.76, f32[2,256]{1,0:T(2,128)S(1)} %fusion.58, bf16[2304,2,128]{0,2,1:T(8,128)(2,1)S(1)} %bitcast.71, bf16[256,2,128]{0,2,1:T(8,128)(2,1)S(1)} %bitcast.83, pred[256,2304]{0,1:T(8,128)(4,1)} %bitcast.79), kind=kOutput, calls=%fused_computation.22 | convolution fusion | flops 609946368 | bytes 3213312 | tf_op jit(solution)/shard_map/hqk,khd->qhd/dot_general | solution.py:48
  173.5 5.2 %all-to-all-start = ((bf16[8,2,256,256]{3,2,1,0:T(8,128)(2,1)}), bf16[8,2,256,256]{3,2,1,0:T(8,128)(2,1)}, u32[]{:S(2)}, u32[]{:S(2)}) async-start(bf16[8,2,256,256]{3,2,1,0:T(8,128)(2,1)} %stack.5), calls=%async_computation | async-start | bytes 4194304 | tf_op jit(solution)/shard_map/all_to_all | solution.py:76
  178.7 2.4 %copy.75 = bf16[8,256,512]{2,1,0:T(8,128)(2,1)} copy(bf16[8,256,512]{1,2,0:T(8,128)(2,1)S(1)} %bitcast.66) | data formatting | bytes 4194304 | tf_op jit(solution)/shard_map/all_to_all | solution.py:73
  181.0 49.8 %all-to-all-done = bf16[8,2,256,256]{3,2,1,0:T(8,128)(2,1)} async-done(((bf16[8,2,256,256]{3,2,1,0:T(8,128)(2,1)}), bf16[8,2,256,256]{3,2,1,0:T(8,128)(2,1)}, u32[]{:S(2)}, u32[]{:S(2)}) %all-to-all-start) | async-done | bytes 2097184 | tf_op jit(solution)/shard_map/all_to_all | solution.py:76
  230.8 2.8 %copy.73 = bf16[2,256,8,256]{3,2,1,0:T(8,128)(2,1)S(1)} copy(bf16[2,256,8,256]{3,1,0,2:T(8,128)(2,1)} %bitcast.16) | data formatting | bytes 4194304 | tf_op jit(solution)/shard_map/reshape | solution.py:77
  235.2 2.0 convolution_convert_fusion
  (80 shorter events, 21.6 us)
Async XLA Ops:
  1.1 18.5 %collective-permute-start = (bf16[2,256,256]{1,2,0:T(8,128)(2,1)S(1)}, bf16[2,256,256]{1,2,0:T(8,128)(2,1)S(1)}, u32[]{:S(2)}, u32[]{:S(2)}) collective-permute-start(bf16[2,256,256]{1,2,0:T(8,128)(2,1)S(1)} %bitcast.77), channel_id=1, source_target_pairs={{0,8},{8,16},{16,24},{24,32},{32,40},{40,48},{48,56},{56,64},{64,7... | collective-permute-start | bytes 786440 | tf_op jit(solution)/shard_map/ppermute | solution.py:15
  19.6 18.4 %copy-start.3 = (bf16[2,256,256]{1,2,0:T(8,128)(2,1)}, bf16[2,256,256]{1,2,0:T(8,128)(2,1)S(1)}, u32[]{:S(2)}) copy-start(bf16[2,256,256]{1,2,0:T(8,128)(2,1)S(1)} %collective-permute-done) | copy-start | bytes 786436
  19.6 12.4 %collective-permute-start.1 = (bf16[2,256,256]{1,2,0:T(8,128)(2,1)S(1)}, bf16[2,256,256]{1,2,0:T(8,128)(2,1)S(1)}, u32[]{:S(2)}, u32[]{:S(2)}) collective-permute-start(bf16[2,256,256]{1,2,0:T(8,128)(2,1)S(1)} %collective-permute-done), channel_id=1, source_target_pairs={{0,8},{8,16},{16,24},{24,32},{32,40},{40,48},{48,56},{56,64},{64,7... | collective-permute-start | bytes 786440 | tf_op jit(solution)/shard_map/ppermute | solution.py:15
  32.0 6.0 %copy-start.5 = (bf16[2,256,256]{1,2,0:T(8,128)(2,1)}, bf16[2,256,256]{1,2,0:T(8,128)(2,1)S(1)}, u32[]{:S(2)}) copy-start(bf16[2,256,256]{1,2,0:T(8,128)(2,1)S(1)} %collective-permute-done.1) | copy-start | bytes 786436
  32.0 12.4 %collective-permute-start.2 = (bf16[2,256,256]{1,2,0:T(8,128)(2,1)S(1)}, bf16[2,256,256]{1,2,0:T(8,128)(2,1)}, u32[]{:S(2)}, u32[]{:S(2)}) collective-permute-start(bf16[2,256,256]{1,2,0:T(8,128)(2,1)S(1)} %collective-permute-done.1), channel_id=1, source_target_pairs={{0,8},{8,16},{16,24},{24,32},{32,40},{40,48},{48,56},{56,64},{64,7... | collective-permute-start | bytes 786440 | tf_op jit(solution)/shard_map/ppermute | solution.py:15
  38.0 65.4 %copy-start.15 = (s32[4,32]{1,0:T(4,128)S(1)}, s32[4,32]{1,0:T(4,128)}, u32[]{:S(2)}) copy-start(s32[4,32]{1,0:T(4,128)} %param.6) | copy-start | bytes 1540
  38.0 78.6 %copy-start.2 = (bf16[2,256,256]{2,1,0:T(8,128)(2,1)S(1)}, bf16[2,256,256]{2,1,0:T(8,128)(2,1)}, u32[]{:S(2)}) copy-start(bf16[2,256,256]{2,1,0:T(8,128)(2,1)} %param.4) | copy-start | bytes 786436
  38.0 93.0 %copy-start.1 = (bf16[2,2,256,256]{3,2,1,0:T(8,128)(2,1)S(1)}, bf16[2,2,256,256]{3,2,1,0:T(8,128)(2,1)}, u32[]{:S(2)}) copy-start(bf16[2,2,256,256]{3,2,1,0:T(8,128)(2,1)} %param.5) | copy-start | bytes 1572868
  38.0 133.9 %all-to-all-start.1 = ((bf16[256,8,512]{0,2,1:T(8,128)(2,1)}), bf16[256,8,512]{0,2,1:T(8,128)(2,1)S(1)}, u32[]{:S(2)}, u32[]{:S(2)}) async-start(bf16[256,8,512]{0,2,1:T(8,128)(2,1)} %bitcast.67), calls=%async_computation.1 | async-start | bytes 4194304 | tf_op jit(solution)/shard_map/all_to_all | solution.py:73
  44.4 57.1 %collective-permute-start.3 = (bf16[2,256,256]{1,2,0:T(8,128)(2,1)}, bf16[2,256,256]{1,2,0:T(8,128)(2,1)S(1)}, u32[]{:S(2)}, u32[]{:S(2)}) collective-permute-start(bf16[2,256,256]{1,2,0:T(8,128)(2,1)} %collective-permute-done.2), channel_id=1, source_target_pairs={{0,8},{8,16},{16,24},{24,32},{32,40},{40,48},{48,56},{56,64},{64,7... | collective-permute-start | bytes 786440 | tf_op jit(solution)/shard_map/ppermute | solution.py:15
  101.5 15.0 %copy-start.7 = (bf16[2,256,256]{1,2,0:T(8,128)(2,1)}, bf16[2,256,256]{1,2,0:T(8,128)(2,1)S(1)}, u32[]{:S(2)}) copy-start(bf16[2,256,256]{1,2,0:T(8,128)(2,1)S(1)} %collective-permute-done.3) | copy-start | bytes 786436
  101.5 13.0 %collective-permute-start.4 = (bf16[2,256,256]{1,2,0:T(8,128)(2,1)S(1)}, bf16[2,256,256]{1,2,0:T(8,128)(2,1)S(1)}, u32[]{:S(2)}, u32[]{:S(2)}) collective-permute-start(bf16[2,256,256]{1,2,0:T(8,128)(2,1)S(1)} %collective-permute-done.3), channel_id=1, source_target_pairs={{0,8},{8,16},{16,24},{24,32},{32,40},{40,48},{48,56},{56,64},{64,7... | collective-permute-start | bytes 786440 | tf_op jit(solution)/shard_map/ppermute | solution.py:15
  114.6 2.0 copy-start.9
  114.6 12.3 %collective-permute-start.5 = (bf16[2,256,256]{1,2,0:T(8,128)(2,1)S(1)}, bf16[2,256,256]{1,2,0:T(8,128)(2,1)}, u32[]{:S(2)}, u32[]{:S(2)}) collective-permute-start(bf16[2,256,256]{1,2,0:T(8,128)(2,1)S(1)} %collective-permute-done.4), channel_id=1, source_target_pairs={{0,8},{8,16},{16,24},{24,32},{32,40},{40,48},{48,56},{56,64},{64,7... | collective-permute-start | bytes 786440 | tf_op jit(solution)/shard_map/ppermute | solution.py:15
  126.9 11.5 %collective-permute-start.6 = (bf16[2,256,256]{1,2,0:T(8,128)(2,1)}, bf16[2,256,256]{1,2,0:T(8,128)(2,1)S(1)}, u32[]{:S(2)}, u32[]{:S(2)}) collective-permute-start(bf16[2,256,256]{1,2,0:T(8,128)(2,1)} %collective-permute-done.5), channel_id=1, source_target_pairs={{0,8},{8,16},{16,24},{24,32},{32,40},{40,48},{48,56},{56,64},{64,7... | collective-permute-start | bytes 786440 | tf_op jit(solution)/shard_map/ppermute | solution.py:15
  131.1 19.6 %copy-start.10 = (bf16[2,256,256]{1,2,0:T(8,128)(2,1)S(1)}, bf16[2,256,256]{1,2,0:T(8,128)(2,1)}, u32[]{:S(2)}) copy-start(bf16[2,256,256]{1,2,0:T(8,128)(2,1)} %copy-done.9) | copy-start | bytes 786436
  131.9 18.7 %copy-start.8 = (bf16[2,256,256]{1,2,0:T(8,128)(2,1)S(1)}, bf16[2,256,256]{1,2,0:T(8,128)(2,1)}, u32[]{:S(2)}) copy-start(bf16[2,256,256]{1,2,0:T(8,128)(2,1)} %copy-done.7) | copy-start | bytes 786436
  138.3 11.3 %collective-permute-start.7 = (bf16[2,256,256]{1,2,0:T(8,128)(2,1)S(1)}, bf16[2,256,256]{1,2,0:T(8,128)(2,1)S(1)}, u32[]{:S(2)}, u32[]{:S(2)}) collective-permute-start(bf16[2,256,256]{1,2,0:T(8,128)(2,1)S(1)} %collective-permute-done.6), channel_id=1, source_target_pairs={{0,8},{8,16},{16,24},{24,32},{32,40},{40,48},{48,56},{56,64},{64,7... | collective-permute-start | bytes 786440 | tf_op jit(solution)/shard_map/ppermute | solution.py:15
  141.1 10.6 %copy-start.6 = (bf16[2,256,256]{1,2,0:T(8,128)(2,1)S(1)}, bf16[2,256,256]{1,2,0:T(8,128)(2,1)}, u32[]{:S(2)}) copy-start(bf16[2,256,256]{1,2,0:T(8,128)(2,1)} %copy-done.5) | copy-start | bytes 786436
  141.2 10.6 %copy-start.4 = (bf16[2,256,256]{1,2,0:T(8,128)(2,1)S(1)}, bf16[2,256,256]{1,2,0:T(8,128)(2,1)}, u32[]{:S(2)}) copy-start(bf16[2,256,256]{1,2,0:T(8,128)(2,1)} %copy-done.3) | copy-start | bytes 786436
  157.6 5.9 %copy-start.11 = (bf16[1,256,256]{1,2,0:T(8,128)(2,1)S(1)}, bf16[1,256,256]{1,2,0:T(8,128)(2,1)}, u32[]{:S(2)}) copy-start(bf16[1,256,256]{1,2,0:T(8,128)(2,1)} %copy.82) | copy-start | bytes 393220
  166.4 4.4 %copy-start.14 = (bf16[2,128,256]{2,1,0:T(8,128)(2,1)S(1)}, bf16[2,128,256]{2,1,0:T(8,128)(2,1)}, u32[]{:S(2)}) copy-start(bf16[2,128,256]{2,1,0:T(8,128)(2,1)} %fusion.16) | copy-start | bytes 393220
  173.5 57.4 %all-to-all-start = ((bf16[8,2,256,256]{3,2,1,0:T(8,128)(2,1)}), bf16[8,2,256,256]{3,2,1,0:T(8,128)(2,1)}, u32[]{:S(2)}, u32[]{:S(2)}) async-start(bf16[8,2,256,256]{3,2,1,0:T(8,128)(2,1)} %stack.5), calls=%async_computation | async-start | bytes 4194304 | tf_op jit(solution)/shard_map/all_to_all | solution.py:76
  233.6 1.6 copy-start
  (2 other events, 2.8 us)
